TPU v7x, 32 devices: a whole 2x2x4 slice. The times are simulated.
32 devices in a mesh: party: 2 (over x), dp: 16 (over z, y, core).
Axes of the slice: x: 2, y: 2, z: 4, core: 2. Of those that a mesh axis runs over, the one named last changes fastest.
Arguments:
- x_share: float32 [2, 8192, 1024], P('party', 'dp'), may hold values from -6 to 6
- w_share: float32 [2, 1024, 2048], P('party', 'dp'), may hold values from -0.1875 to 0.1875
- g_share: float32 [2, 8192, 2048], P('party', 'dp'), may hold values from -0.0625 to 0.0625
- fwd_a: float32 [2, 8192, 1024], P('party', 'dp'), may hold values from -4 to 4
- fwd_b: float32 [2, 1024, 2048], P('party', 'dp'), may hold values from -0.125 to 0.125
- fwd_c: float32 [2, 8192, 2048], P('party', 'dp'), may hold values from -2100 to 2100, as said below
- bwd_a: float32 [2, 8192, 1024], P('party', 'dp'), may hold values from -4 to 4
- bwd_b: float32 [2, 8192, 2048], P('party', 'dp'), may hold values from -0.044194174 to 0.044194174
- bwd_c: float32 [2, 1024, 2048], P('party', 'dp'), may hold values from -2100 to 2100, as said below
Outputs:
- y_share: float32 [2, 8192, 2048], P('party', 'dp')
- dw_share: float32 [2, 1024, 2048], P('party', 'dp')
Inputs may be any that keep to these rules, and one draw needn't show every extreme that they name: fwd_c[0] + fwd_c[1] equals (fwd_a[0] + fwd_a[1]) (fwd_b[0] + fwd_b[1]) up to float32 rounding. bwd_c[0] + bwd_c[1] equals (bwd_a[0] + bwd_a[1])^T (bwd_b[0] + bwd_b[1]) up to float32 rounding.
All inputs are finite; a program needn't handle non-finite values.
Results may differ from a plain program's by a relative error of at most 0.0001.
Values sent between devices are 32-bit elements; how exact they have to be, the bound alone decides.
A program may use at most 128 MiB of HBM per device.

v0:
```python
import jax
import jax.numpy as jnp
from jax import lax
from jax.sharding import PartitionSpec as P


def matmul(left, right):
    return jnp.dot(left, right, preferred_element_type=jnp.float32, precision=lax.Precision.HIGHEST)


def tmatmul(left, right):
    return lax.dot_general(
        left,
        right,
        (((0,), (0,)), ((), ())),
        precision=lax.Precision.HIGHEST,
        preferred_element_type=jnp.float32,
    )


def body(x_share, w_share, g_share, fwd_a, fwd_b, fwd_c, bwd_a, bwd_b, bwd_c):
    first = (lax.axis_index("party") == 0).astype(jnp.float32)
    inputs = x_share[0]
    left_fwd = fwd_a[0]
    eps_fwd = lax.psum(inputs - left_fwd, "party")
    delta_rows = lax.psum(w_share[0] - fwd_b[0], "party")
    corrected_fwd, delta_fwd = (
        lax.all_gather(fwd_b[0] + first * delta_rows, "dp", axis=0, tiled=True),
        lax.all_gather(delta_rows, "dp", axis=0, tiled=True),
    )
    outputs = fwd_c[0] + matmul(eps_fwd, corrected_fwd) + matmul(left_fwd, delta_fwd)
    left_bwd = bwd_a[0]
    eps_bwd, delta_bwd = lax.psum((inputs - left_bwd, g_share[0] - bwd_b[0]), "party")
    corrected = bwd_b[0] + first * delta_bwd
    partial_value = tmatmul(eps_bwd, corrected) + tmatmul(left_bwd, delta_bwd)
    summed = lax.psum_scatter(partial_value, "dp", scatter_dimension=0, tiled=True)
    return (outputs[None], (bwd_c[0] + summed)[None])


def solution(mesh):
    in_specs = (
        P("party", "dp", None),
        P("party", "dp", None),
        P("party", "dp", None),
        P("party", "dp", None),
        P("party", "dp", None),
        P("party", "dp", None),
        P("party", "dp", None),
        P("party", "dp", None),
        P("party", "dp", None),
    )
    out_specs = (P("party", "dp", None), P("party", "dp", None))
    return jax.shard_map(body, mesh=mesh, in_specs=in_specs, out_specs=out_specs, check_vma=False)
```

profile of v0, /device:TPU:0, one launch (start us, length us, event | category | flops | bytes accessed | tf_op | source)
XLA Modules:
  0.0 543.7 jit_solution(15295625302415227886)
XLA Ops:
  7.2 0.0 all-reduce.3.cloned.1.call-start
  7.2 0.0 copy-start.2
  7.3 6.7 %bitcast_subtract_fusion = f32[512,2048]{1,0:T(8,128)} fusion(f32[1,512,2048]{2,1,0:T(8,128)} %param.11, f32[1,512,2048]{2,1,0:T(8,128)} %param.16), kind=kLoop, calls=%fused_computation.1 | loop fusion | flops 1048576 | bytes 12582912 | tf_op jit(solution)/shard_map/sub | solution.py:33
  14.0 0.0 copy-done.7
  14.0 0.8 bitcast_subtract_fusion.3
  14.8 2.7 bitcast_subtract_fusion.1
  17.6 0.0 all-reduce.3.cloned.1.call-update
  17.6 0.0 reduce-scatter.2.cloned.1.call-start
  17.6 212.2 %all-reduce.3.cloned.1.call-done = (f32[512,1024]{1,0:T(8,128)}, f32[64,2048]{1,0:T(8,128)}, f32[512,1024]{1,0:T(8,128)}, f32[512,2048]{1,0:T(8,128)}) async-done(((f32[512,1024]{1,0:T(8,128)}, f32[64,2048]{1,0:T(8,128)}, f32[512,1024]{1,0:T(8,128)}, f32[512,2048]{1,0:T(8,128)}), (f32[512,1024]{1,0:T(8,128)}, f32[64,2048]{1,0:T(8,128)}, f32[512,1024]{1,0:T(8,128)}, ...) | async-done | bytes 8912912 | tf_op jit(solution)/shard_map/psum | solution.py:25
  229.9 17.6 %fusion = f32[1024,2048]{1,0:T(8,128)S(1)} fusion(f32[512,1024]{1,0:T(8,128)} %get-tuple-element.4, f32[1,512,2048]{2,1,0:T(8,128)} %param.16, f32[512,2048]{1,0:T(8,128)} %get-tuple-element.5, f32[]{:T(128)S(6)} %convert_element_type.3), kind=kOutput, calls=%fused_computation.3 | convolution fusion | flops 12886999040 | bytes 18874372 | tf_op jit(solution)/shard_map/dot_general | solution.py:12
  247.5 16.4 %bitcast_add_fusion = f32[1024,2048]{1,0:T(8,128)} fusion(f32[1024,2048]{1,0:T(8,128)S(1)} %fusion, f32[512,2048]{1,0:T(8,128)S(1)} %copy-done, f32[1,512,1024]{2,1,0:T(8,128)S(1)} %copy-done.1), kind=kOutput, calls=%fused_computation | convolution fusion | flops 12886999040 | bytes 23068672 | tf_op jit(solution)/shard_map/dot_general | solution.py:12
  263.9 0.0 reduce-scatter.2.cloned.1.call-update
  263.9 0.0 all-gather.3.cloned.1.call-start
  264.0 1.0 copy-done.6
  264.9 0.8 bitcast_add_fusion.6
  265.8 0.0 all-gather.3.cloned.1.call-update
  265.8 0.0 all-gather.5.cloned.1.call-start
  265.9 0.5 all-gather.5.cloned.1.call-update
  266.4 101.8 %reduce-scatter.2.cloned.1.call-done = f32[64,2048]{1,0:T(8,128)} async-done(((f32[1024,2048]{1,0:T(8,128)}), f32[64,2048]{1,0:T(8,128)}) %reduce-scatter.2.cloned.1.call-update) | async-done | bytes 524304 | tf_op jit(solution)/shard_map/reduce_scatter | solution.py:36
  368.2 1.9 fusion.6
  370.1 74.8 %all-gather.3.cloned.1.call-done = f32[1024,2048]{1,0:T(8,128)} async-done(((f32[64,2048]{1,0:T(8,128)}), f32[1024,2048]{1,0:T(8,128)}) %all-gather.3.cloned.1.call-update) | async-done | bytes 8388624 | tf_op jit(solution)/shard_map/all_gather | solution.py:28
  444.9 18.1 %fusion.7 = f32[512,2048]{1,0:T(8,128)} fusion(f32[512,1024]{1,0:T(8,128)} %get-tuple-element.2, f32[1024,2048]{1,0:T(8,128)} %all-gather.3.cloned.1.call-done), kind=kOutput, calls=%fused_computation.17 | convolution fusion | flops 12884901888 | bytes 14680064 | tf_op jit(solution)/shard_map/dot_general | solution.py:8
  463.1 56.8 %all-gather.5.cloned.1.call-done = f32[1024,2048]{1,0:T(8,128)} async-done(((f32[64,2048]{1,0:T(8,128)}), f32[1024,2048]{1,0:T(8,128)}) %all-gather.5.cloned.1.call-update) | async-done | bytes 8388624 | tf_op jit(solution)/shard_map/all_gather | solution.py:29
  519.9 17.3 %fusion.1 = f32[1,512,2048]{2,1,0:T(8,128)} fusion(f32[512,2048]{1,0:T(8,128)} %fusion.7, f32[1,512,2048]{2,1,0:T(8,128)} %param.14, f32[1024,2048]{1,0:T(8,128)} %all-gather.5.cloned.1.call-done, f32[1,512,1024]{2,1,0:T(8,128)S(1)} %copy-done.3), kind=kOutput, calls=%fused_computation.5 | convolution fusion | flops 12886999040 | bytes 23068672 | tf_op jit(solution)/shard_map/dot_general | solution.py:8
  (15 shorter events, 0.0 us)
Async XLA Ops:
  7.2 6.8 %copy-start.7 = (f32[1,64,2048]{2,1,0:T(8,128)S(1)}, f32[1,64,2048]{2,1,0:T(8,128)}, u32[]{:S(2)}) copy-start(f32[1,64,2048]{2,1,0:T(8,128)} %param.10) | copy-start | bytes 1572868
  7.2 6.8 %copy-start.5 = (f32[1,64,2048]{2,1,0:T(8,128)S(1)}, f32[1,64,2048]{2,1,0:T(8,128)}, u32[]{:S(2)}) copy-start(f32[1,64,2048]{2,1,0:T(8,128)} %param.13) | copy-start | bytes 1572868
  7.2 7.6 %copy-start.1 = (f32[1,512,1024]{2,1,0:T(8,128)S(1)}, f32[1,512,1024]{2,1,0:T(8,128)}, u32[]{:S(2)}) copy-start(f32[1,512,1024]{2,1,0:T(8,128)} %param.15) | copy-start | bytes 6291460
  7.2 222.7 %all-reduce.3.cloned.1.call-start = ((), (), s32[]{:S(2)}) async-start(), calls=%async_computation.4 | async-start | bytes 17825792 | tf_op jit(solution)/shard_map/psum | solution.py:25
  7.2 7.6 %copy-start.2 = (f32[1,512,1024]{2,1,0:T(8,128)S(1)}, f32[1,512,1024]{2,1,0:T(8,128)}, u32[]{:S(2)}) copy-start(f32[1,512,1024]{2,1,0:T(8,128)} %param.12) | copy-start | bytes 6291460
  7.3 7.6 %copy-start.4 = (f32[1,512,1024]{2,1,0:T(8,128)S(1)}, f32[1,512,1024]{2,1,0:T(8,128)}, u32[]{:S(2)}) copy-start(f32[1,512,1024]{2,1,0:T(8,128)} %param.9) | copy-start | bytes 6291460
  17.6 350.6 %reduce-scatter.2.cloned.1.call-start = ((), (), s32[]{:S(2)}) async-start(), calls=%async_computation.3 | async-start | bytes 8912896 | tf_op jit(solution)/shard_map/reduce_scatter | solution.py:36
  229.8 17.7 %copy-start = (f32[512,2048]{1,0:T(8,128)S(1)}, f32[512,2048]{1,0:T(8,128)}, u32[]{:S(2)}) copy-start(f32[512,2048]{1,0:T(8,128)} %get-tuple-element.5) | copy-start | bytes 12582916
  263.9 1.0 copy-start.6
  263.9 104.3 %copy-start.8 = (f32[1,64,2048]{2,1,0:T(8,128)S(1)}, f32[1,64,2048]{2,1,0:T(8,128)}, u32[]{:S(2)}) copy-start(f32[1,64,2048]{2,1,0:T(8,128)} %param.17) | copy-start | bytes 1572868
  263.9 181.0 %all-gather.3.cloned.1.call-start = ((), (), s32[]{:S(2)}) async-start(), calls=%async_computation.1 | async-start | bytes 8912896 | tf_op jit(solution)/shard_map/all_gather | solution.py:28
  265.8 254.0 %all-gather.5.cloned.1.call-start = ((), (), s32[]{:S(2)}) async-start(), calls=%async_computation.2 | async-start | bytes 8912896 | tf_op jit(solution)/shard_map/all_gather | solution.py:29
  444.9 74.9 %copy-start.3 = (f32[1,512,1024]{2,1,0:T(8,128)S(1)}, f32[1,512,1024]{2,1,0:T(8,128)}, u32[]{:S(2)}) copy-start(f32[1,512,1024]{2,1,0:T(8,128)} %param.12) | copy-start | bytes 6291460
Sparse Core Ops, SparseCore 0:
  17.7 212.1 all-reduce.2
  264.1 104.1 reduce-scatter.1
  371.0 73.9 all-gather.2
  447.0 72.8 all-gather.4
where the time goes:
time: 544 us
  waiting for transfers between devices  446 us (82%)
  matrix products  69.5 us (13%)
  between operations  13.8 us (3%)
  other arithmetic  13 us (2%)
    psum x1, waiting for transfers between devices, body(): eps_fwd = lax.psum(inputs - left_fwd, 'party')  212 us
    reduce_scatter x1, waiting for transfers between devices, body(): lax.psum_scatter(partial_value, 'dp', scatter_dimension=0, tiled=True)  102 us
    all_gather x1, waiting for transfers between devices, body(): lax.all_gather(fwd_b[0] + first * delta_rows, 'dp', axis=0, tiled=True)  74.8 us
    all_gather x1, waiting for transfers between devices, body(): lax.all_gather(delta_rows, 'dp', axis=0, tiled=True)  56.8 us
    dot_general x2, matrix products, matmul(): jnp.dot(left, right, preferred_element_type=jnp.float32, precision=lax.Pr...  35.4 us
    dot_general x2, matrix products, tmatmul(): lax.dot_general(left, right, (((0,), (0,)), ((), ())), precision=lax.Prec...  34 us
  transfers between devices with their start and end apart: 4, of which 4 were waited for; matrix products, arithmetic and copies ran while one was open for 4% of the time, Pallas kernels for 0%

commit v1 on v0

--- a/solution.py
+++ b/solution.py
@@ -22,7 +22,7 @@
     first = (lax.axis_index("party") == 0).astype(jnp.float32)
     inputs = x_share[0]
     left_fwd = fwd_a[0]
-    eps_fwd = lax.psum(inputs - left_fwd, "party")
+    eps_fwd = jnp.sum(lax.all_gather(inputs - left_fwd, "party"), axis=0)
     delta_rows = lax.psum(w_share[0] - fwd_b[0], "party")
     corrected_fwd, delta_fwd = (
         lax.all_gather(fwd_b[0] + first * delta_rows, "dp", axis=0, tiled=True),

time: 544 us -> 527 us (0.969)
  waiting for transfers between devices: 446 us -> 423 us
    psum x1, waiting for transfers between devices: 212 us -> 164 us  [body(): delta_rows = lax.psum(w_share[0] - fwd_b[0], 'party')]
    all_gather x0 -> x1, waiting for transfers between devices: none -> 21.3 us  [body(): eps_fwd = jnp.sum(lax.all_gather(inputs - left_fwd, 'party'), axis=0)]
  transfers between devices with their start and end apart: 4 -> 5, of which waited for: 4 -> 5; matrix products, arithmetic and copies ran while one was open for 4% -> 12% of each run, Pallas kernels for 0% -> 0%
where the time goes in v1:
time: 527 us; the launch traced here: 526 us
  waiting for transfers between devices  423 us (80%)
  matrix products  70 us (13%)
  other arithmetic  18.2 us (3%)
  between operations  13.8 us (3%)
    psum x1, waiting for transfers between devices, body(): delta_rows = lax.psum(w_share[0] - fwd_b[0], 'party')  164 us
    reduce_scatter x1, waiting for transfers between devices, body(): lax.psum_scatter(partial_value, 'dp', scatter_dimension=0, tiled=True)  105 us
    all_gather x1, waiting for transfers between devices, body(): lax.all_gather(fwd_b[0] + first * delta_rows, 'dp', axis=0, tiled=True)  74.7 us
    all_gather x1, waiting for transfers between devices, body(): lax.all_gather(delta_rows, 'dp', axis=0, tiled=True)  57.6 us
    dot_general x2, matrix products, matmul(): jnp.dot(left, right, preferred_element_type=jnp.float32, precision=lax.Pr...  35.6 us
    dot_general x2, matrix products, tmatmul(): lax.dot_general(left, right, (((0,), (0,)), ((), ())), precision=lax.Prec...  34.4 us
    all_gather x1, waiting for transfers between devices, body(): eps_fwd = jnp.sum(lax.all_gather(inputs - left_fwd, 'party'), axis=0)  21.3 us
  transfers between devices with their start and end apart: 5, of which 5 were waited for; matrix products, arithmetic and copies ran while one was open for 12% of the time, Pallas kernels for 0%

profile of v1, /device:TPU:0, one launch (start us, length us, event | category | flops | bytes accessed | tf_op | source)
XLA Modules:
  0.0 526.3 jit_solution(15168326984914676289)
XLA Ops:
  7.2 0.0 all-reduce.3.cloned.1.call-start
  7.2 6.7 %bitcast_subtract_fusion = f32[512,2048]{1,0:T(8,128)} fusion(f32[1,512,2048]{2,1,0:T(8,128)} %param.11, f32[1,512,2048]{2,1,0:T(8,128)} %param.16), kind=kLoop, calls=%fused_computation.1 | loop fusion | flops 1048576 | bytes 12582912 | tf_op jit(solution)/shard_map/sub | solution.py:33
  14.0 1.7 bitcast_subtract_fusion.1
  15.7 0.9 bitcast_subtract_fusion.2
  16.6 0.0 all-reduce.3.cloned.1.call-update
  16.6 0.0 all-gather.4.cloned.1.call-start
  16.6 3.3 sub.13
  20.0 0.0 reduce-scatter.2.cloned.1.call-start
  20.1 164.0 %all-reduce.3.cloned.1.call-done = (f32[64,2048]{1,0:T(8,128)}, f32[512,1024]{1,0:T(8,128)}, f32[512,2048]{1,0:T(8,128)}) async-done(((f32[64,2048]{1,0:T(8,128)}, f32[512,1024]{1,0:T(8,128)}, f32[512,2048]{1,0:T(8,128)}), (f32[64,2048]{1,0:T(8,128)}, f32[512,1024]{1,0:T(8,128)}, f32[512,2048]{1,0:T(8,128)})) %all-reduce.3.cloned.1.call-update) | async-done | bytes 6815760 | tf_op jit(solution)/shard_map/psum | solution.py:26
  184.1 17.6 %fusion = f32[1024,2048]{1,0:T(8,128)S(1)} fusion(f32[512,1024]{1,0:T(8,128)} %get-tuple-element.3, f32[1,512,2048]{2,1,0:T(8,128)} %param.16, f32[512,2048]{1,0:T(8,128)} %get-tuple-element.4, f32[]{:T(128)S(6)} %convert_element_type.3), kind=kOutput, calls=%fused_computation.3 | convolution fusion | flops 12886999040 | bytes 18874372 | tf_op jit(solution)/shard_map/dot_general | solution.py:12
  201.7 16.8 %bitcast_add_fusion = f32[1024,2048]{1,0:T(8,128)} fusion(f32[1024,2048]{1,0:T(8,128)S(1)} %fusion, f32[512,2048]{1,0:T(8,128)S(1)} %copy-done, f32[1,512,1024]{2,1,0:T(8,128)S(1)} %copy-done.3), kind=kOutput, calls=%fused_computation | convolution fusion | flops 12886999040 | bytes 23068672 | tf_op jit(solution)/shard_map/dot_general | solution.py:12
  218.6 0.0 all-gather.6.cloned.1.call-start
  218.6 1.0 copy-done.5
  219.6 0.8 bitcast_add_fusion.6
  220.4 0.0 all-gather.8.cloned.1.call-start
  220.5 0.5 all-gather.8.cloned.1.call-update
  221.0 21.3 %all-gather.4.cloned.1.call-done = f32[2,512,1024]{2,1,0:T(8,128)} async-done(((f32[1,512,1024]{2,1,0:T(8,128)}), f32[2,512,1024]{2,1,0:T(8,128)}) %all-gather.4.cloned.1.call-update) | async-done | bytes 4194320 | tf_op jit(solution)/shard_map/all_gather | solution.py:25
  242.4 2.8 reduce_sum.9
  245.2 104.7 %reduce-scatter.2.cloned.1.call-done = f32[64,2048]{1,0:T(8,128)} async-done(((f32[1024,2048]{1,0:T(8,128)}), f32[64,2048]{1,0:T(8,128)}) %reduce-scatter.2.cloned.1.call-update) | async-done | bytes 524304 | tf_op jit(solution)/shard_map/reduce_scatter | solution.py:36
  349.9 1.9 fusion.6
  351.8 74.7 %all-gather.6.cloned.1.call-done = f32[1024,2048]{1,0:T(8,128)} async-done(((f32[64,2048]{1,0:T(8,128)}), f32[1024,2048]{1,0:T(8,128)}) %all-gather.6.cloned.1.call-update) | async-done | bytes 8388624 | tf_op jit(solution)/shard_map/all_gather | solution.py:28
  426.5 17.3 %fusion.7 = f32[512,2048]{1,0:T(8,128)} fusion(f32[512,1024]{1,0:T(8,128)S(1)} %reduce_sum.9, f32[1024,2048]{1,0:T(8,128)} %all-gather.6.cloned.1.call-done), kind=kOutput, calls=%fused_computation.16 | convolution fusion | flops 12884901888 | bytes 14680064 | tf_op jit(solution)/shard_map/dot_general | solution.py:8
  443.8 57.6 %all-gather.8.cloned.1.call-done = f32[1024,2048]{1,0:T(8,128)} async-done(((f32[64,2048]{1,0:T(8,128)}), f32[1024,2048]{1,0:T(8,128)}) %all-gather.8.cloned.1.call-update) | async-done | bytes 8388624 | tf_op jit(solution)/shard_map/all_gather | solution.py:29
  501.4 18.3 %fusion.1 = f32[1,512,2048]{2,1,0:T(8,128)} fusion(f32[512,2048]{1,0:T(8,128)} %fusion.7, f32[1,512,2048]{2,1,0:T(8,128)} %param.14, f32[1024,2048]{1,0:T(8,128)} %all-gather.8.cloned.1.call-done, f32[1,512,1024]{2,1,0:T(8,128)} %param.12), kind=kOutput, calls=%fused_computation.5 | convolution fusion | flops 12886999040 | bytes 23068672 | tf_op jit(solution)/shard_map/dot_general | solution.py:8
  (18 shorter events, 0.1 us)
Async XLA Ops:
  7.2 6.8 %copy-start.1 = (f32[1,512,1024]{2,1,0:T(8,128)S(1)}, f32[1,512,1024]{2,1,0:T(8,128)}, u32[]{:S(2)}) copy-start(f32[1,512,1024]{2,1,0:T(8,128)} %param.9) | copy-start | bytes 6291460
  7.2 176.9 %all-reduce.3.cloned.1.call-start = ((), (), s32[]{:S(2)}) async-start(), calls=%async_computation.5 | async-start | bytes 13631488 | tf_op jit(solution)/shard_map/psum | solution.py:26
  7.2 6.7 %copy-start.2 = (f32[1,512,1024]{2,1,0:T(8,128)S(1)}, f32[1,512,1024]{2,1,0:T(8,128)}, u32[]{:S(2)}) copy-start(f32[1,512,1024]{2,1,0:T(8,128)} %param.15) | copy-start | bytes 6291460
  13.9 1.8 copy-start.4
  13.9 1.8 copy-start.6
  16.6 225.8 %all-gather.4.cloned.1.call-start = ((), (), s32[]{:S(2)}) async-start(), calls=%async_computation.1 | async-start | bytes 6291456 | tf_op jit(solution)/shard_map/all_gather | solution.py:25
  20.0 329.9 %reduce-scatter.2.cloned.1.call-start = ((), (), s32[]{:S(2)}) async-start(), calls=%async_computation.4 | async-start | bytes 8912896 | tf_op jit(solution)/shard_map/reduce_scatter | solution.py:36
  184.1 17.7 %copy-start = (f32[512,2048]{1,0:T(8,128)S(1)}, f32[512,2048]{1,0:T(8,128)}, u32[]{:S(2)}) copy-start(f32[512,2048]{1,0:T(8,128)} %get-tuple-element.4) | copy-start | bytes 12582916
  184.1 17.7 %copy-start.3 = (f32[1,512,1024]{2,1,0:T(8,128)S(1)}, f32[1,512,1024]{2,1,0:T(8,128)}, u32[]{:S(2)}) copy-start(f32[1,512,1024]{2,1,0:T(8,128)} %param.15) | copy-start | bytes 6291460
  218.5 1.0 copy-start.5
  218.6 207.9 %all-gather.6.cloned.1.call-start = ((), (), s32[]{:S(2)}) async-start(), calls=%async_computation.2 | async-start | bytes 8912896 | tf_op jit(solution)/shard_map/all_gather | solution.py:28
  220.4 129.5 %copy-start.7 = (f32[1,64,2048]{2,1,0:T(8,128)S(1)}, f32[1,64,2048]{2,1,0:T(8,128)}, u32[]{:S(2)}) copy-start(f32[1,64,2048]{2,1,0:T(8,128)} %param.17) | copy-start | bytes 1572868
  220.4 281.0 %all-gather.8.cloned.1.call-start = ((), (), s32[]{:S(2)}) async-start(), calls=%async_computation.3 | async-start | bytes 8912896 | tf_op jit(solution)/shard_map/all_gather | solution.py:29
Sparse Core Ops, SparseCore 0:
  16.7 167.3 all-reduce.2
  185.6 56.7 all-gather.3
  246.4 103.4 reduce-scatter.1
  352.5 73.9 all-gather.5
  428.5 72.8 all-gather.7
